TPU v7x, 32 devices: a whole 2x2x4 slice. The times are simulated.
32 devices in a mesh: fsdp: 2 (over x), ctx: 4 (over z), tp: 4 (over y, core).
Axes of the slice: x: 2, y: 2, z: 4, core: 2. Of those that a mesh axis runs over, the one named last changes fastest.
Arguments:
- inputs: bfloat16 [2, 1024, 1024], P('fsdp', 'ctx'), may hold values from -6 to 6
- upstream: bfloat16 [2, 1024, 1024], P('fsdp', 'ctx'), may hold values from -6 to 6
- teacher: bfloat16 [2, 1024, 1024], P('fsdp', 'ctx'), may hold values from -8 to 8
- valid: int32 [2, 1024], P('fsdp', 'ctx'), may hold values from 0 to 1, as said below
- segment: int32 [2, 1024], P('fsdp', 'ctx'), may hold values from 0 to 7, never falling along the last dimension, each value on 1 to 512 neighbouring positions
- gain_one: float32 [1024], replicated, may hold values from 0.25 to 1.75
- query_weight: bfloat16 [1024, 1024], P('fsdp', 'tp'), may hold values from -0.1875 to 0.1875
- key_weight: bfloat16 [1024, 1024], P('fsdp', 'tp'), may hold values from -0.1875 to 0.1875
- value_weight: bfloat16 [1024, 1024], P('fsdp', 'tp'), may hold values from -0.1875 to 0.1875
- out_weight: bfloat16 [1024, 1024], P('tp', 'fsdp'), may hold values from -0.75 to 0.75
- gain_two: float32 [1024], replicated, may hold values from 0.25 to 1.75
- gate_weight: bfloat16 [1024, 2816], P('fsdp', 'tp'), may hold values from -0.1875 to 0.1875
- up_weight: bfloat16 [1024, 2816], P('fsdp', 'tp'), may hold values from -0.1875 to 0.1875
- down_weight: bfloat16 [2816, 1024], P('tp', 'fsdp'), may hold values from -0.21875 to 0.21875
Outputs:
- output: bfloat16 [2, 1024, 1024], P('fsdp', 'ctx')
- loss: float32 [2], replicated
- grad_inputs: float32 [2, 1024, 1024], P('fsdp', 'ctx')
- grad_gain_one: float32 [1024], P('fsdp')
- grad_query: float32 [1024, 1024], P('fsdp', 'tp')
- grad_key: float32 [1024, 1024], P('fsdp', 'tp')
- grad_value: float32 [1024, 1024], P('fsdp', 'tp')
- grad_out: float32 [1024, 1024], P('tp', 'fsdp')
- grad_gain_two: float32 [1024], P('fsdp')
- grad_gate: float32 [1024, 2816], P('fsdp', 'tp')
- grad_up: float32 [1024, 2816], P('fsdp', 'tp')
- grad_down: float32 [2816, 1024], P('tp', 'fsdp')
Inputs may be any that keep to these rules, and one draw needn't show every extreme that they name: `segment`: segment numbers never fall along a sequence; each document has 1 to 512 positions and one has exactly 512. The first token of every sequence is valid.
All inputs are finite; a program needn't handle non-finite values.
Results may differ from a plain program's by a relative error of at most 0.018.
Values may be sent and summed in bfloat16 or wider, within the bound.
A program may use at most 128 MiB of HBM per device.

v0:
```python
import jax
import jax.numpy as jnp
from jax import lax
from jax.sharding import PartitionSpec as P

HEAD_DIM = 64


def rms_scale(values_in, scales_in):
    return (
        values_in
        * lax.rsqrt(jnp.mean(values_in * values_in, axis=-1, keepdims=True) + 1e-05)
        * scales_in
    )


def swiglu(gate_act, up_act):
    return jax.nn.silu(gate_act) * up_act


def head_total(partial_sum):
    return lax.psum(partial_sum, "tp")


def contract(left, right, pattern):
    return jnp.einsum(pattern, left, right, preferred_element_type=jnp.float32)


def shards(
    inputs,
    upstream,
    teacher,
    valid,
    segment,
    gain_one,
    query_weight,
    key_weight,
    value_weight,
    out_weight,
    gain_two,
    gate_weight,
    up_weight,
    down_weight,
):
    seq_dev, ctx_tok, width = inputs.shape
    row_count = seq_dev * ctx_tok
    head_cols = query_weight.shape[1]
    heads_here = head_cols // HEAD_DIM
    scaling = HEAD_DIM ** (-0.5)
    full_query, full_key, full_value, full_gate, full_up = (
        lax.all_gather(query_weight, "fsdp", axis=0, tiled=True),
        lax.all_gather(key_weight, "fsdp", axis=0, tiled=True),
        lax.all_gather(value_weight, "fsdp", axis=0, tiled=True),
        lax.all_gather(gate_weight, "fsdp", axis=0, tiled=True),
        lax.all_gather(up_weight, "fsdp", axis=0, tiled=True),
    )
    full_out, full_down = (
        lax.all_gather(out_weight, "fsdp", axis=1, tiled=True),
        lax.all_gather(down_weight, "fsdp", axis=1, tiled=True),
    )
    seg_whole = lax.all_gather(segment, "ctx", axis=1, tiled=True)
    seq_len = seg_whole.shape[1]
    query_places = lax.axis_index("ctx") * ctx_tok + jnp.arange(ctx_tok, dtype=jnp.int32)
    key_places = jnp.arange(seq_len, dtype=jnp.int32)
    causal = key_places[None, :] <= query_places[:, None]
    flat_in = inputs.reshape(row_count, width).astype(jnp.float32)
    normed_one = rms_scale(flat_in, gain_one).astype(jnp.bfloat16)
    queries = jnp.dot(normed_one, full_query, preferred_element_type=jnp.float32).astype(
        jnp.bfloat16
    )
    keys_low = jnp.dot(normed_one, full_key, preferred_element_type=jnp.float32).astype(
        jnp.bfloat16
    )
    values_low = jnp.dot(normed_one, full_value, preferred_element_type=jnp.float32).astype(
        jnp.bfloat16
    )
    pairs = jnp.concatenate([keys_low, values_low], axis=1).reshape(seq_dev, ctx_tok, 2 * head_cols)
    pairs_all = lax.all_gather(pairs, "ctx", axis=1, tiled=True)
    query_heads = queries.reshape(seq_dev, ctx_tok, heads_here, HEAD_DIM)

    def scores_of(query_one, pairs_one, seg_all, seg_own):
        keys_one = pairs_one[:, :head_cols].reshape(seq_len, heads_here, HEAD_DIM)
        values_one = pairs_one[:, head_cols:].reshape(seq_len, heads_here, HEAD_DIM)
        allowed = causal & (seg_all[None, :] == seg_own[:, None])
        raw_scores = contract(query_one, keys_one, "qhd,khd->hqk") * scaling
        masked = jnp.where(allowed[None], raw_scores, -1e30)
        return (keys_one, values_one, allowed, masked)

    def attend_forward(bundle):
        query_one, pairs_one, seg_all, seg_own = bundle
        keys_one, values_one, allowed, masked = scores_of(query_one, pairs_one, seg_all, seg_own)
        top_score = jnp.max(masked, axis=-1, keepdims=True)
        exponent = jnp.where(allowed[None], jnp.exp(masked - top_score), 0.0)
        denominator = jnp.sum(exponent, axis=-1, keepdims=True)
        probs_low = (exponent / denominator).astype(jnp.bfloat16)
        mixed_one = contract(probs_low, values_one, "hqk,khd->qhd")
        return (mixed_one, top_score + jnp.log(denominator))

    mixed, log_norm = lax.map(attend_forward, (query_heads, pairs_all, seg_whole, segment))
    mixed_low = mixed.reshape(row_count, head_cols).astype(jnp.bfloat16)
    middle = flat_in + head_total(jnp.dot(mixed_low, full_out, preferred_element_type=jnp.float32))
    normed_two = rms_scale(middle, gain_two).astype(jnp.bfloat16)
    gate_low = jnp.dot(normed_two, full_gate, preferred_element_type=jnp.float32).astype(
        jnp.bfloat16
    )
    up_low = jnp.dot(normed_two, full_up, preferred_element_type=jnp.float32).astype(jnp.bfloat16)
    gate_wide = gate_low.astype(jnp.float32)
    up_wide = up_low.astype(jnp.float32)
    hidden_low = swiglu(gate_wide, up_wide).astype(jnp.bfloat16)
    result = middle + head_total(jnp.dot(hidden_low, full_down, preferred_element_type=jnp.float32))
    weighting = valid.reshape(row_count, 1).astype(jnp.float32)
    differ = result - teacher.reshape(row_count, width).astype(jnp.float32)
    per_sequence = jnp.sum((weighting * differ * differ).reshape(seq_dev, ctx_tok * width), axis=1)
    all_seqs = seq_dev * lax.axis_size("fsdp")
    own_seqs = lax.axis_index("fsdp") * seq_dev + jnp.arange(seq_dev, dtype=jnp.int32)
    placed = jnp.sum(
        jnp.where(
            own_seqs[:, None] == jnp.arange(all_seqs, dtype=jnp.int32)[None, :],
            per_sequence[:, None],
            0.0,
        ),
        axis=0,
    )
    counted, squared = lax.psum((jnp.sum(weighting), placed), ("fsdp", "ctx"))
    loss_value = squared * all_seqs / (counted * width)
    cotangent = upstream.reshape(row_count, width).astype(jnp.float32) + weighting * differ
    branch_grad = cotangent.astype(jnp.bfloat16)
    grad_down = contract(hidden_low, branch_grad, "rf,rd->fd")
    hidden_grad = contract(branch_grad, full_down, "rd,fd->rf")
    ignored, swiglu_back = jax.vjp(swiglu, gate_wide, up_wide)
    gate_grad, up_grad = swiglu_back(hidden_grad)
    gate_grad = gate_grad.astype(jnp.bfloat16)
    up_grad = up_grad.astype(jnp.bfloat16)
    grad_gate = contract(normed_two, gate_grad, "rd,rf->df")
    grad_up = contract(normed_two, up_grad, "rd,rf->df")
    norm_two_grad = head_total(
        contract(gate_grad, full_gate, "rf,df->rd") + contract(up_grad, full_up, "rf,df->rd")
    )
    ignored, norm_two_back = jax.vjp(rms_scale, middle, gain_two)
    middle_part, grad_gain_two = norm_two_back(norm_two_grad)
    middle_grad = cotangent + middle_part
    attn_grad = middle_grad.astype(jnp.bfloat16)
    grad_out = contract(mixed_low, attn_grad, "rh,rd->hd")
    mixed_grad = (
        contract(attn_grad, full_out, "rd,hd->rh")
        .astype(jnp.bfloat16)
        .reshape(seq_dev, ctx_tok, heads_here, HEAD_DIM)
    )

    def attend_backward(bundle):
        query_one, pairs_one, seg_all, seg_own, lse_one, grad_one = bundle
        keys_one, values_one, allowed, masked = scores_of(query_one, pairs_one, seg_all, seg_own)
        prob_full = jnp.where(allowed[None], jnp.exp(masked - lse_one), 0.0)
        value_grad = contract(prob_full.astype(jnp.bfloat16), grad_one, "hqk,qhd->khd")
        prob_grad = contract(grad_one, values_one, "qhd,khd->hqk")
        score_grad = (
            prob_full * (prob_grad - jnp.sum(prob_full * prob_grad, axis=-1, keepdims=True))
        ).astype(jnp.bfloat16)
        query_grad = contract(score_grad, keys_one, "hqk,khd->qhd") * scaling
        key_grad = contract(score_grad, query_one, "hqk,qhd->khd") * scaling
        return (
            query_grad,
            jnp.concatenate(
                [key_grad.reshape(seq_len, head_cols), value_grad.reshape(seq_len, head_cols)],
                axis=1,
            ),
        )

    query_grads, pair_terms = lax.map(
        attend_backward, (query_heads, pairs_all, seg_whole, segment, log_norm, mixed_grad)
    )
    pair_grads = (
        lax.psum_scatter(pair_terms, "ctx", scatter_dimension=1, tiled=True)
        .astype(jnp.bfloat16)
        .reshape(row_count, 2 * head_cols)
    )
    query_low = query_grads.reshape(row_count, head_cols).astype(jnp.bfloat16)
    key_low = pair_grads[:, :head_cols]
    value_low = pair_grads[:, head_cols:]
    grad_query = contract(normed_one, query_low, "rd,rh->dh")
    grad_key = contract(normed_one, key_low, "rd,rh->dh")
    grad_value = contract(normed_one, value_low, "rd,rh->dh")
    norm_one_grad = head_total(
        contract(query_low, full_query, "rh,dh->rd")
        + contract(key_low, full_key, "rh,dh->rd")
        + contract(value_low, full_value, "rh,dh->rd")
    )
    ignored, norm_one_back = jax.vjp(rms_scale, flat_in, gain_one)
    input_part, grad_gain_one = norm_one_back(norm_one_grad)
    grad_inputs = (middle_grad + input_part).reshape(seq_dev, ctx_tok, width)
    row_query, row_key, row_value, row_gate, row_up, row_one, row_two = (
        lax.psum_scatter(
            grad_query.astype(jnp.bfloat16), "fsdp", scatter_dimension=0, tiled=True
        ).astype(jnp.float32),
        lax.psum_scatter(
            grad_key.astype(jnp.bfloat16), "fsdp", scatter_dimension=0, tiled=True
        ).astype(jnp.float32),
        lax.psum_scatter(
            grad_value.astype(jnp.bfloat16), "fsdp", scatter_dimension=0, tiled=True
        ).astype(jnp.float32),
        lax.psum_scatter(
            grad_gate.astype(jnp.bfloat16), "fsdp", scatter_dimension=0, tiled=True
        ).astype(jnp.float32),
        lax.psum_scatter(
            grad_up.astype(jnp.bfloat16), "fsdp", scatter_dimension=0, tiled=True
        ).astype(jnp.float32),
        lax.psum_scatter(
            grad_gain_one.astype(jnp.bfloat16), "fsdp", scatter_dimension=0, tiled=True
        ).astype(jnp.float32),
        lax.psum_scatter(
            grad_gain_two.astype(jnp.bfloat16), "fsdp", scatter_dimension=0, tiled=True
        ).astype(jnp.float32),
    )
    col_out, col_down = (
        lax.psum_scatter(
            grad_out.astype(jnp.bfloat16), "fsdp", scatter_dimension=1, tiled=True
        ).astype(jnp.float32),
        lax.psum_scatter(
            grad_down.astype(jnp.bfloat16), "fsdp", scatter_dimension=1, tiled=True
        ).astype(jnp.float32),
    )
    sum_query, sum_key, sum_value, sum_gate, sum_up, sum_one, sum_two, sum_out, sum_down = (
        lax.psum(row_query.astype(jnp.bfloat16), "ctx").astype(jnp.float32),
        lax.psum(row_key.astype(jnp.bfloat16), "ctx").astype(jnp.float32),
        lax.psum(row_value.astype(jnp.bfloat16), "ctx").astype(jnp.float32),
        lax.psum(row_gate.astype(jnp.bfloat16), "ctx").astype(jnp.float32),
        lax.psum(row_up.astype(jnp.bfloat16), "ctx").astype(jnp.float32),
        lax.psum(row_one.astype(jnp.bfloat16), "ctx").astype(jnp.float32),
        lax.psum(row_two.astype(jnp.bfloat16), "ctx").astype(jnp.float32),
        lax.psum(col_out.astype(jnp.bfloat16), "ctx").astype(jnp.float32),
        lax.psum(col_down.astype(jnp.bfloat16), "ctx").astype(jnp.float32),
    )
    output = result.astype(jnp.bfloat16).reshape(seq_dev, ctx_tok, width)
    return (
        output,
        loss_value,
        grad_inputs,
        sum_one,
        sum_query,
        sum_key,
        sum_value,
        sum_out,
        sum_two,
        sum_gate,
        sum_up,
        sum_down,
    )


def solution(mesh):
    placed = (
        P("fsdp", "ctx", None),
        P("fsdp", "ctx", None),
        P("fsdp", "ctx", None),
        P("fsdp", "ctx"),
        P("fsdp", "ctx"),
        P(),
        P("fsdp", "tp"),
        P("fsdp", "tp"),
        P("fsdp", "tp"),
        P("tp", "fsdp"),
        P(),
        P("fsdp", "tp"),
        P("fsdp", "tp"),
        P("tp", "fsdp"),
    )
    return jax.shard_map(
        shards,
        mesh=mesh,
        in_specs=placed,
        out_specs=(
            P("fsdp", "ctx", None),
            P(),
            P("fsdp", "ctx", None),
            P("fsdp"),
            P("fsdp", "tp"),
            P("fsdp", "tp"),
            P("fsdp", "tp"),
            P("tp", "fsdp"),
            P("fsdp"),
            P("fsdp", "tp"),
            P("fsdp", "tp"),
            P("tp", "fsdp"),
        ),
        check_vma=False,
    )
```

profile of v0, /device:TPU:0, one launch (start us, length us, event | category | flops | bytes accessed | tf_op | source)
XLA Modules:
  0.0 628.7 jit_solution(3718089470991618106)
XLA Ops:
  8.1 1.3 fusion.18
  9.4 10.2 %all_gather.29 = bf16[1024,256]{1,0:T(8,128)(2,1)S(1)} all-gather(bf16[512,256]{1,0:T(8,128)(2,1)} %param.21), channel_id=1, replica_groups=mesh['fsdp'=2,'ctx'=4,'tp'=4] {'fsdp'}, dimensions={0}, use_global_device_ids=true | all-gather | bytes 786432 | tf_op jit(solution)/shard_map/all_gather | solution.py:52
  19.6 8.3 %all_gather.30 = bf16[1024,256]{1,0:T(8,128)(2,1)S(1)} all-gather(bf16[512,256]{1,0:T(8,128)(2,1)} %param.22), channel_id=1, replica_groups=mesh['fsdp'=2,'ctx'=4,'tp'=4] {'fsdp'}, dimensions={0}, use_global_device_ids=true | all-gather | bytes 786432 | tf_op jit(solution)/shard_map/all_gather | solution.py:53
  28.0 1.7 convolution_convert_fusion.12
  29.7 1.5 convolution_convert_fusion.11
  32.0 11.1 %all_gather.32 = s32[1,1024]{1,0:T(1,128)S(1)} all-gather(s32[1,256]{1,0:T(1,128)S(1)} %copy-done.47), channel_id=1, replica_groups=mesh['fsdp'=2,'ctx'=4,'tp'=4] {'ctx'}, dimensions={1}, use_global_device_ids=true | all-gather | bytes 5120 | tf_op jit(solution)/shard_map/all_gather | solution.py:61
  43.1 8.5 %all_gather.34 = bf16[1024,256]{1,0:T(8,128)(2,1)S(1)} all-gather(bf16[512,256]{1,0:T(8,128)(2,1)S(1)} %copy-done.34), channel_id=1, replica_groups=mesh['fsdp'=2,'ctx'=4,'tp'=4] {'fsdp'}, dimensions={0}, use_global_device_ids=true | all-gather | bytes 786432 | tf_op jit(solution)/shard_map/all_gather | solution.py:51
  51.5 7.0 %all_gather.35 = bf16[256,1024]{1,0:T(8,128)(2,1)S(1)} all-gather(bf16[256,512]{1,0:T(8,128)(2,1)S(1)} %copy-done.35), channel_id=1, replica_groups=mesh['fsdp'=2,'ctx'=4,'tp'=4] {'fsdp'}, dimensions={1}, use_global_device_ids=true | all-gather | bytes 786432 | tf_op jit(solution)/shard_map/all_gather | solution.py:58
  59.4 3.8 all-gather.12.cloned.1.call-done
  63.2 1.3 fusion.58
  65.2 1.0 fusion.1
  66.2 1.5 fusion
  68.3 1.8 fusion.15
  70.7 1.3 fusion.59
  73.9 33.0 %all-reduce.12.cloned.1.call-done = f32[256,1024]{1,0:T(8,128)} async-done(((f32[256,1024]{1,0:T(8,128)}), f32[256,1024]{1,0:T(8,128)}) %all-reduce.12.cloned.1.call-update) | async-done | bytes 1048592 | tf_op jit(solution)/shard_map/psum | solution.py:22
  106.8 1.5 multiply_reduce_fusion.3
  108.5 3.0 fusion.13
  111.5 13.5 %all-gather.8.cloned.1.call-done = bf16[1024,704]{0,1:T(8,128)(2,1)} async-done(((bf16[512,704]{0,1:T(8,128)(2,1)}), bf16[1024,704]{0,1:T(8,128)(2,1)}) %all-gather.8.cloned.1.call-update) | async-done | bytes 1441808 | tf_op jit(solution)/shard_map/all_gather | solution.py:55
  125.0 3.0 multiply_convert_fusion.3
  128.0 24.0 %all-gather.10.cloned.1.call-done = bf16[704,1024]{1,0:T(8,128)(2,1)} async-done(((bf16[704,512]{1,0:T(8,128)(2,1)}), bf16[704,1024]{1,0:T(8,128)(2,1)}) %all-gather.10.cloned.1.call-update) | async-done | bytes 1441808 | tf_op jit(solution)/shard_map/all_gather | solution.py:59
  152.0 2.9 fusion.60
  155.1 36.4 %all-reduce.14.cloned.1.call-done = f32[256,1024]{1,0:T(8,128)} async-done(((f32[256,1024]{1,0:T(8,128)}), f32[256,1024]{1,0:T(8,128)}) %all-reduce.14.cloned.1.call-update) | async-done | bytes 1048592 | tf_op jit(solution)/shard_map/psum | solution.py:22
  191.4 1.8 multiply_add_fusion
  193.5 2.3 multiply_convert_fusion.2
  196.7 1.6 convolution_add_fusion.2
  199.2 36.0 %all-reduce.16.cloned.1.call-done = f32[256,1024]{1,0:T(8,128)} async-done(((f32[256,1024]{1,0:T(8,128)}), f32[256,1024]{1,0:T(8,128)}) %all-reduce.16.cloned.1.call-update) | async-done | bytes 1048592 | tf_op jit(solution)/shard_map/psum | solution.py:22
  235.2 3.4 multiply_reduce_fusion.1
  239.3 1.5 fusion.23
  241.2 1.3 fusion.2
  242.5 1.9 multiply_reduce_fusion
  244.4 1.4 multiply_convert_fusion
  246.3 1.5 maximum_bitcast_fusion
  247.9 2.1 convolution_convert_fusion.3
  250.0 1.8 fusion.14
  252.5 2.3 convolution_convert_fusion.6
  254.9 2.9 convolution_convert_fusion.2
  257.9 1.6 convolution_convert_fusion
  259.6 1.6 convolution_convert_fusion.1
  261.4 30.8 %reduce-scatter.9.cloned.1.call-done = f32[1,256,512]{1,2,0:T(8,128)} async-done(((f32[1,1024,512]{1,2,0:T(8,128)}), f32[1,256,512]{1,2,0:T(8,128)}) %reduce-scatter.9.cloned.1.call-update) | async-done | bytes 524304 | tf_op jit(solution)/shard_map/reduce_scatter | solution.py:173
  292.1 1.1 convert_bitcast_fusion.2
  293.2 1.2 convolution_convert_fusion.5
  294.5 1.2 convolution_convert_fusion.4
  296.6 1.3 convolution_add_fusion
  298.0 10.0 %reduce-scatter.17.cloned.1.call-done = bf16[256,512]{1,0:T(8,128)(2,1)} async-done(((bf16[256,1024]{1,0:T(8,128)(2,1)}), bf16[256,512]{1,0:T(8,128)(2,1)}) %reduce-scatter.17.cloned.1.call-update) | async-done | bytes 262160 | tf_op jit(solution)/shard_map/reduce_scatter | solution.py:215
  308.1 17.5 %reduce-scatter.11.cloned.1.call-done = bf16[512,256]{1,0:T(8,128)(2,1)} async-done(((bf16[1024,256]{1,0:T(8,128)(2,1)}), bf16[512,256]{1,0:T(8,128)(2,1)}) %reduce-scatter.11.cloned.1.call-update) | async-done | bytes 262160 | tf_op jit(solution)/shard_map/reduce_scatter | solution.py:192
  325.6 27.6 %reduce-scatter.23.cloned.1.call-done = bf16[704,512]{1,0:T(8,128)(2,1)} async-done(((bf16[704,1024]{1,0:T(8,128)(2,1)}), bf16[704,512]{1,0:T(8,128)(2,1)}) %reduce-scatter.23.cloned.1.call-update) | async-done | bytes 720912 | tf_op jit(solution)/shard_map/reduce_scatter | solution.py:218
  353.1 27.6 %reduce-scatter.21.cloned.1.call-done = bf16[512,704]{0,1:T(8,128)(2,1)} async-done(((bf16[1024,704]{0,1:T(8,128)(2,1)}), bf16[512,704]{0,1:T(8,128)(2,1)}) %reduce-scatter.21.cloned.1.call-update) | async-done | bytes 720912 | tf_op jit(solution)/shard_map/reduce_scatter | solution.py:204
  380.7 27.4 %reduce-scatter.19.cloned.1.call-done = bf16[512,704]{0,1:T(8,128)(2,1)} async-done(((bf16[1024,704]{0,1:T(8,128)(2,1)}), bf16[512,704]{0,1:T(8,128)(2,1)}) %reduce-scatter.19.cloned.1.call-update) | async-done | bytes 720912 | tf_op jit(solution)/shard_map/reduce_scatter | solution.py:201
  408.1 17.5 %reduce-scatter.13.cloned.1.call-done = bf16[512,256]{1,0:T(8,128)(2,1)} async-done(((bf16[1024,256]{1,0:T(8,128)(2,1)}), bf16[512,256]{1,0:T(8,128)(2,1)}) %reduce-scatter.13.cloned.1.call-update) | async-done | bytes 262160 | tf_op jit(solution)/shard_map/reduce_scatter | solution.py:195
  425.6 17.3 %reduce-scatter.15.cloned.1.call-done = bf16[512,256]{1,0:T(8,128)(2,1)} async-done(((bf16[1024,256]{1,0:T(8,128)(2,1)}), bf16[512,256]{1,0:T(8,128)(2,1)}) %reduce-scatter.15.cloned.1.call-update) | async-done | bytes 262160 | tf_op jit(solution)/shard_map/reduce_scatter | solution.py:198
  445.5 21.2 %all-reduce.2 = (f32[2]{0:T(128)S(1)}, f32[]{:T(128)}) all-reduce(f32[2]{0:T(128)S(1)} %compare_select_fusion, f32[]{:T(128)} %convert_reduce_fusion), channel_id=1, replica_groups=mesh['fsdp'=2,'ctx'=4,'tp'=4] {'fsdp','ctx'}, use_global_device_ids=true, to_apply=%region_7.8 | all-reduce | flops 3 | bytes 24 | tf_op jit(solution)/shard_map/psum | solution.py:124
  467.8 14.4 %all-reduce.18.cloned.1.call-done = f32[256,1024]{1,0:T(8,128)} async-done(((f32[256,1024]{1,0:T(8,128)}), f32[256,1024]{1,0:T(8,128)}) %all-reduce.18.cloned.1.call-update) | async-done | bytes 1048592 | tf_op jit(solution)/shard_map/psum | solution.py:22
  482.2 1.6 fusion.17
  483.8 4.9 all-reduce.5
  488.9 12.3 %all-reduce.3 = (bf16[512]{0:T(512)(128)(2,1)S(1)}, bf16[512]{0:T(512)(128)(2,1)S(1)}) all-reduce(bf16[512]{0:T(512)(128)(2,1)S(1)} %dynamic-slice.2, bf16[512]{0:T(512)(128)(2,1)S(1)} %dynamic-slice.4), channel_id=1, replica_groups=mesh['fsdp'=2,'ctx'=4,'tp'=4] {'ctx'}, use_global_device_ids=true, to_apply=%region_18.19 | all-reduce | flops 1024 | bytes 4096 | tf_op jit(solution)/shard_map/psum | solution.py:228
  502.3 2.5 fusion.25
  504.8 104.2 %all-reduce.20.cloned.1.call-done = (bf16[512,256]{1,0:T(8,128)(2,1)}, bf16[512,256]{1,0:T(8,128)(2,1)}, bf16[512,256]{1,0:T(8,128)(2,1)}, bf16[256,512]{1,0:T(8...) async-done(((bf16[512,256]{1,0:T(8,128)(2,1)}, bf16[512,256]{1,0:T(8,128)(2,1)}, bf16[512,256]{1,0:T(8,128)(2,1)}, ...) | async-done | bytes 3211280 | tf_op jit(solution)/shard_map/psum | solution.py:223
  609.1 1.9 convert_element_type.237
  610.9 1.8 convert_element_type.239
  612.7 1.8 convert_element_type.241
  614.5 1.8 convert_element_type.243
  616.3 2.4 convert_element_type.247
  618.7 1.3 convert_element_type.249
  620.0 1.3 convert_element_type.251
  (163 shorter events, 14.8 us)
Async XLA Ops:
  8.0 50.9 %copy-start.3 = (bf16[1,256,1024]{2,1,0:T(8,128)(2,1)S(1)}, bf16[1,256,1024]{2,1,0:T(8,128)(2,1)}, u32[]{:S(2)}) copy-start(bf16[1,256,1024]{2,1,0:T(8,128)(2,1)} %param.14) | copy-start | bytes 1572868
  8.0 50.9 %copy-start.37 = (f32[1024]{0:T(1024)S(1)}, f32[1024]{0:T(1024)}, u32[]{:S(2)}) copy-start(f32[1024]{0:T(1024)} %param.19) | copy-start | bytes 12292
  8.0 23.9 %copy-start.47 = (s32[1,256]{1,0:T(1,128)S(1)}, s32[1,256]{1,0:T(1,128)}, u32[]{:S(2)}) copy-start(s32[1,256]{1,0:T(1,128)} %param.18) | copy-start | bytes 3076
  8.0 35.0 %copy-start.34 = (bf16[512,256]{1,0:T(8,128)(2,1)S(1)}, bf16[512,256]{1,0:T(8,128)(2,1)}, u32[]{:S(2)}) copy-start(bf16[512,256]{1,0:T(8,128)(2,1)} %param.20) | copy-start | bytes 786436
  8.1 43.5 %copy-start.35 = (bf16[256,512]{1,0:T(8,128)(2,1)S(1)}, bf16[256,512]{1,0:T(8,128)(2,1)}, u32[]{:S(2)}) copy-start(bf16[256,512]{1,0:T(8,128)(2,1)} %param.23) | copy-start | bytes 786436
  8.1 55.1 %all-gather.12.cloned.1.call-start = ((), (), s32[]{:S(2)}) async-start(), calls=%async_computation.23 | async-start | bytes 1310720 | tf_op jit(solution)/shard_map/all_gather | solution.py:78
  9.4 22.6 %copy-start.41 = (f32[256]{0:T(256)}, f32[256]{0:T(256)S(1)}, u32[]{:S(2)}) copy-start(f32[256]{0:T(256)S(1)} %fusion.18) | copy-start | bytes 3076
  9.4 49.9 %copy-start.44 = (f32[256]{0:T(256)}, f32[256]{0:T(256)S(1)}, u32[]{:S(2)}) copy-start(f32[256]{0:T(256)S(1)} %fusion.44) | copy-start | bytes 3076
  19.6 8.3 %copy-start.17 = (bf16[1024,256]{1,0:T(8,128)(2,1)}, bf16[1024,256]{1,0:T(8,128)(2,1)S(1)}, u32[]{:S(2)}) copy-start(bf16[1024,256]{1,0:T(8,128)(2,1)S(1)} %all_gather.29) | copy-start | bytes 1572868
  28.0 15.1 %copy-start.15 = (bf16[1024,256]{1,0:T(8,128)(2,1)}, bf16[1024,256]{1,0:T(8,128)(2,1)S(1)}, u32[]{:S(2)}) copy-start(bf16[1024,256]{1,0:T(8,128)(2,1)S(1)} %all_gather.30) | copy-start | bytes 1572868
  31.9 74.9 %all-reduce.12.cloned.1.call-start = ((), (), s32[]{:S(2)}) async-start(), calls=%async_computation.8 | async-start | bytes 2097152 | tf_op jit(solution)/shard_map/psum | solution.py:22
  51.5 7.3 %copy-start.13 = (bf16[1024,256]{1,0:T(8,128)(2,1)}, bf16[1024,256]{1,0:T(8,128)(2,1)S(1)}, u32[]{:S(2)}) copy-start(bf16[1024,256]{1,0:T(8,128)(2,1)S(1)} %all_gather.34) | copy-start | bytes 1572868
  58.6 11.5 %copy-start.8 = (bf16[256,1024]{1,0:T(8,128)(2,1)}, bf16[256,1024]{1,0:T(8,128)(2,1)S(1)}, u32[]{:S(2)}) copy-start(bf16[256,1024]{1,0:T(8,128)(2,1)S(1)} %all_gather.35) | copy-start | bytes 1572868
  64.4 3.3 copy-start.29
  66.2 3.9 copy-start
  70.1 38.2 %copy-start.36 = (f32[1024]{0:T(1024)S(1)}, f32[1024]{0:T(1024)}, u32[]{:S(2)}) copy-start(f32[1024]{0:T(1024)} %param.24) | copy-start | bytes 12292
  72.1 36.5 %all-gather.6.cloned.1.call-start = ((), (), s32[]{:S(2)}) async-start(), calls=%async_computation.9 | async-start | bytes 2162688 | tf_op jit(solution)/shard_map/all_gather | solution.py:54
  72.6 52.4 %all-gather.8.cloned.1.call-start = ((), (), s32[]{:S(2)}) async-start(), calls=%async_computation.10 | async-start | bytes 2162688 | tf_op jit(solution)/shard_map/all_gather | solution.py:55
  73.2 78.8 %all-gather.10.cloned.1.call-start = ((), (), s32[]{:S(2)}) async-start(), calls=%async_computation.11 | async-start | bytes 2162688 | tf_op jit(solution)/shard_map/all_gather | solution.py:59
  73.8 117.6 %all-reduce.14.cloned.1.call-start = ((), (), s32[]{:S(2)}) async-start(), calls=%async_computation.12 | async-start | bytes 2097152 | tf_op jit(solution)/shard_map/psum | solution.py:22
  108.3 19.7 %copy-start.43 = (f32[256]{0:T(256)}, f32[256]{0:T(256)S(1)}, u32[]{:S(2)}) copy-start(f32[256]{0:T(256)S(1)} %get-tuple-element.84) | copy-start | bytes 3076
  108.5 46.5 %copy-start.5 = (bf16[256,1024]{1,0:T(8,128)(2,1)}, bf16[256,1024]{1,0:T(8,128)(2,1)S(1)}, u32[]{:S(2)}) copy-start(bf16[256,1024]{1,0:T(8,128)(2,1)S(1)} %multiply_convert_fusion.1) | copy-start | bytes 1572868
  111.5 43.5 %copy-start.48 = (s32[1,256]{1,0:T(1,128)S(1)}, s32[1,256]{1,0:T(1,128)}, u32[]{:S(2)}) copy-start(s32[1,256]{1,0:T(1,128)} %param.17) | copy-start | bytes 3076
  111.5 79.9 %copy-start.12 = (bf16[1,256,1024]{2,1,0:T(8,128)(2,1)S(1)}, bf16[1,256,1024]{2,1,0:T(8,128)(2,1)}, u32[]{:S(2)}) copy-start(bf16[1,256,1024]{2,1,0:T(8,128)(2,1)} %param.16) | copy-start | bytes 1572868
  128.0 63.5 %copy-start.23 = (bf16[256,704]{0,1:T(8,128)(2,1)}, bf16[256,704]{0,1:T(8,128)(2,1)S(1)}, u32[]{:S(2)}) copy-start(bf16[256,704]{0,1:T(8,128)(2,1)S(1)} %get-tuple-element.93) | copy-start | bytes 1081348
  155.0 80.2 %all-reduce.16.cloned.1.call-start = ((), (), s32[]{:S(2)}) async-start(), calls=%async_computation.13 | async-start | bytes 2097152 | tf_op jit(solution)/shard_map/psum | solution.py:22
  155.1 40.8 %copy-start.40 = (f32[1,256]{1,0:T(1,128)}, f32[1,256]{1,0:T(1,128)S(1)}, u32[]{:S(2)}) copy-start(f32[1,256]{1,0:T(1,128)S(1)} %convert_element_type.214) | copy-start | bytes 3076
  191.4 1.8 copy-start.21
  191.4 2.0 copy-start.51
  193.2 46.0 %copy-start.2 = (f32[256,1024]{1,0:T(8,128)}, f32[256,1024]{1,0:T(8,128)S(1)}, u32[]{:S(2)}) copy-start(f32[256,1024]{1,0:T(8,128)S(1)} %multiply_add_fusion) | copy-start | bytes 3145732
  193.2 2.6 copy-start.7
  193.5 3.2 copy-start.22
  195.8 0.8 copy-start.25
  195.8 39.3 %copy-start.11 = (f32[256,1024]{1,0:T(8,128)S(1)}, f32[256,1024]{1,0:T(8,128)}, u32[]{:S(2)}) copy-start(f32[256,1024]{1,0:T(8,128)} %all-reduce.14.cloned.1.call-done) | copy-start | bytes 3145732
  198.3 93.8 %reduce-scatter.9.cloned.1.call-start = ((), (), s32[]{:S(2)}) async-start(), calls=%async_computation.14 | async-start | bytes 2621440 | tf_op jit(solution)/shard_map/reduce_scatter | solution.py:173
  235.2 5.6 copy-start.9
  235.2 6.0 copy-start.1
  241.1 1.3 copy-start.30
  247.8 4.7 copy-start.38
  247.8 4.7 copy-start.45
  247.8 7.0 %copy-start.24 = (bf16[256,704]{0,1:T(8,128)(2,1)S(1)}, bf16[256,704]{0,1:T(8,128)(2,1)}, u32[]{:S(2)}) copy-start(bf16[256,704]{0,1:T(8,128)(2,1)} %copy-done.23) | copy-start | bytes 1081348
  247.9 60.2 %reduce-scatter.17.cloned.1.call-start = ((), (), s32[]{:S(2)}) async-start(), calls=%async_computation.19 | async-start | bytes 786432 | tf_op jit(solution)/shard_map/reduce_scatter | solution.py:215
  250.0 75.6 %reduce-scatter.11.cloned.1.call-start = ((), (), s32[]{:S(2)}) async-start(), calls=%async_computation.16 | async-start | bytes 786432 | tf_op jit(solution)/shard_map/reduce_scatter | solution.py:192
  251.8 6.0 copy-start.6
  251.9 6.0 copy-start.26
  254.8 4.9 copy-start.20
  254.8 98.3 %reduce-scatter.23.cloned.1.call-start = ((), (), s32[]{:S(2)}) async-start(), calls=%async_computation.22 | async-start | bytes 2162688 | tf_op jit(solution)/shard_map/reduce_scatter | solution.py:218
  257.8 35.4 %copy-start.4 = (bf16[1,256,1024]{2,1,0:T(8,128)(2,1)S(1)}, bf16[1,256,1024]{2,1,0:T(8,128)(2,1)}, u32[]{:S(2)}) copy-start(bf16[1,256,1024]{2,1,0:T(8,128)(2,1)} %param.14) | copy-start | bytes 1572868
  257.8 122.8 %reduce-scatter.21.cloned.1.call-start = ((), (), s32[]{:S(2)}) async-start(), calls=%async_computation.21 | async-start | bytes 2162688 | tf_op jit(solution)/shard_map/reduce_scatter | solution.py:204
  259.6 36.3 %copy-start.14 = (bf16[1024,256]{1,0:T(8,128)(2,1)S(1)}, bf16[1024,256]{1,0:T(8,128)(2,1)}, u32[]{:S(2)}) copy-start(bf16[1024,256]{1,0:T(8,128)(2,1)} %copy-done.13) | copy-start | bytes 1572868
  259.6 36.3 %copy-start.33 = (bf16[4,64,256]{2,1,0:T(8,128)(2,1)S(1)}, bf16[4,64,256]{2,1,0:T(8,128)(2,1)}, u32[]{:S(2)}) copy-start(bf16[4,64,256]{2,1,0:T(8,128)(2,1)} %copy-done.32) | copy-start | bytes 393220
  259.6 148.5 %reduce-scatter.19.cloned.1.call-start = ((), (), s32[]{:S(2)}) async-start(), calls=%async_computation.20 | async-start | bytes 2162688 | tf_op jit(solution)/shard_map/reduce_scatter | solution.py:201
  261.3 34.9 %copy-start.18 = (bf16[1024,256]{1,0:T(8,128)(2,1)S(1)}, bf16[1024,256]{1,0:T(8,128)(2,1)}, u32[]{:S(2)}) copy-start(bf16[1024,256]{1,0:T(8,128)(2,1)} %copy-done.17) | copy-start | bytes 1572868
  261.3 164.3 %reduce-scatter.13.cloned.1.call-start = ((), (), s32[]{:S(2)}) async-start(), calls=%async_computation.17 | async-start | bytes 786432 | tf_op jit(solution)/shard_map/reduce_scatter | solution.py:195
  293.2 3.4 copy-start.16
  294.5 148.4 %reduce-scatter.15.cloned.1.call-start = ((), (), s32[]{:S(2)}) async-start(), calls=%async_computation.18 | async-start | bytes 786432 | tf_op jit(solution)/shard_map/reduce_scatter | solution.py:198
  295.8 186.4 %all-reduce.18.cloned.1.call-start = ((), (), s32[]{:S(2)}) async-start(), calls=%async_computation.15 | async-start | bytes 2097152 | tf_op jit(solution)/shard_map/psum | solution.py:22
  296.6 146.4 %copy-start.50 = (u32[32]{0:T(128)S(1)}, u32[32]{0:T(128)}, u32[]{:S(2)}) copy-start(u32[32]{0:T(128)} %constant.94) | copy-start | bytes 388
  296.6 146.9 %copy-start.49 = (s32[1,256]{1,0:T(1,128)S(1)}, s32[1,256]{1,0:T(1,128)}, u32[]{:S(2)}) copy-start(s32[1,256]{1,0:T(1,128)} %param.17) | copy-start | bytes 3076
  296.6 187.2 %copy-start.46 = (bf16[1024]{0:T(1024)(128)(2,1)S(1)}, bf16[1024]{0:T(1024)(128)(2,1)}, u32[]{:S(2)}) copy-start(bf16[1024]{0:T(1024)(128)(2,1)} %get-tuple-element.56) | copy-start | bytes 6148
  296.6 205.7 %copy-start.42 = (f32[256]{0:T(256)S(1)}, f32[256]{0:T(256)}, u32[]{:S(2)}) copy-start(f32[256]{0:T(256)} %copy-done.41) | copy-start | bytes 3076
  298.0 311.1 %all-reduce.20.cloned.1.call-start = ((), (), s32[]{:S(2)}) async-start(), calls=%async_computation.24 | async-start | bytes 6422528 | tf_op jit(solution)/shard_map/psum | solution.py:223
  609.1 9.7 %copy-start.28 = (bf16[512,704]{0,1:T(8,128)(2,1)S(1)}, bf16[512,704]{0,1:T(8,128)(2,1)}, u32[]{:S(2)}) copy-start(bf16[512,704]{0,1:T(8,128)(2,1)} %get-tuple-element.80) | copy-start | bytes 2162692
  609.1 11.0 %copy-start.27 = (bf16[704,512]{1,0:T(8,128)(2,1)S(1)}, bf16[704,512]{1,0:T(8,128)(2,1)}, u32[]{:S(2)}) copy-start(bf16[704,512]{1,0:T(8,128)(2,1)} %get-tuple-element.81) | copy-start | bytes 2162692
  (5 other events, 3.4 us)
Sparse Core Ops, SparseCore 0:
  32.0 31.0 all-gather.11
  72.2 34.5 all-reduce.11
  155.1 36.2 all-reduce.13
  198.4 36.7 all-reduce.15
  248.0 44.0 reduce-scatter.8
  294.2 13.8 reduce-scatter.16
  310.9 14.6 reduce-scatter.10
  328.4 24.6 reduce-scatter.22
  355.9 24.6 reduce-scatter.20
  383.3 24.6 reduce-scatter.18
  410.9 14.6 reduce-scatter.12
  428.2 14.6 reduce-scatter.14
  445.9 36.3 all-reduce.17
  485.0 124.0 all-reduce.19
Sparse Core Ops, SparseCore 1:
  74.1 23.8 all-gather.5
  99.4 25.5 all-gather.7
  126.4 25.5 all-gather.9
where the time goes:
time: 630 us; the launch traced here: 629 us
  waiting for transfers between devices  443 us (70%)
  blocking collectives  83.5 us (13%)
  matrix products  42 us (7%)
  other arithmetic  36.8 us (6%)
  between operations  17.6 us (3%)
    psum x4, waiting for transfers between devices, head_total(): return lax.psum(partial_sum, 'tp')  120 us
    psum x1, waiting for transfers between devices, shards(): lax.psum(row_query.astype(jnp.bfloat16), 'ctx').astype(jnp.float32)  104 us
    reduce_scatter x1, waiting for transfers between devices, shards(): lax.psum_scatter(pair_terms, 'ctx', scatter_dimension=1, tiled=True)  30.8 us
    dot_general x20, matrix products, contract(): return jnp.einsum(pattern, left, right, preferred_element_type=jnp.float32)  28.2 us
    reduce_scatter x1, waiting for transfers between devices, shards(): lax.psum_scatter(grad_up.astype(jnp.bfloat16), 'fsdp', scatter_dimension=...  27.6 us
    reduce_scatter x1, waiting for transfers between devices, shards(): lax.psum_scatter(grad_down.astype(jnp.bfloat16), 'fsdp', scatter_dimensio...  27.6 us
    reduce_scatter x1, waiting for transfers between devices, shards(): lax.psum_scatter(grad_gate.astype(jnp.bfloat16), 'fsdp', scatter_dimensio...  27.4 us
    all_gather x1, waiting for transfers between devices, shards(): lax.all_gather(down_weight, 'fsdp', axis=1, tiled=True)  24 us
  transfers between devices with their start and end apart: 17, of which 16 were waited for; matrix products, arithmetic and copies ran while one was open for 6% of the time, Pallas kernels for 0%

commit v1 on v0

--- a/solution.py
+++ b/solution.py
@@ -4,6 +4,20 @@
 from jax.sharding import PartitionSpec as P
 
 HEAD_DIM = 64
+
+
+def patch_measure(matrix, peer_axis):
+    carry_in, t1 = (jax.lax.psum(1, peer_axis), jax.lax.axis_index(peer_axis))
+    current_block, side_arr = (matrix, 1)
+    while side_arr < carry_in:
+        moved = jax.lax.ppermute(
+            current_block, peer_axis, [(to_i, to_i ^ side_arr) for to_i in range(carry_in)]
+        )
+        low = jnp.concatenate([current_block, moved], axis=0)
+        z_new = jnp.concatenate([moved, current_block], axis=0)
+        current_block = jnp.where(t1 & side_arr == 0, low, z_new)
+        side_arr = 2 * side_arr
+    return current_block
 
 
 def rms_scale(values_in, scales_in):
@@ -52,7 +66,7 @@
         lax.all_gather(key_weight, "fsdp", axis=0, tiled=True),
         lax.all_gather(value_weight, "fsdp", axis=0, tiled=True),
         lax.all_gather(gate_weight, "fsdp", axis=0, tiled=True),
-        lax.all_gather(up_weight, "fsdp", axis=0, tiled=True),
+        patch_measure(up_weight, "fsdp"),
     )
     full_out, full_down = (
         lax.all_gather(out_weight, "fsdp", axis=1, tiled=True),

time: 630 us -> 608 us (0.965)
  waiting for transfers between devices: 443 us -> 421 us
    all_gather x1 -> x0, waiting for transfers between devices: 13.5 us -> none  [shards(): lax.all_gather(up_weight, 'fsdp', axis=0, tiled=True)]
    all_gather x1, waiting for transfers between devices: 24 us -> 16 us  [shards(): lax.all_gather(down_weight, 'fsdp', axis=1, tiled=True)]
    reduce_scatter x1, waiting for transfers between devices: 10 us -> 16.9 us  [shards(): lax.psum_scatter(grad_out.astype(jnp.bfloat16), 'fsdp', scatter_dimension...]
    reduce_scatter x1, waiting for transfers between devices: 17.5 us -> 10.6 us  [shards(): lax.psum_scatter(grad_query.astype(jnp.bfloat16), 'fsdp', scatter_dimensi...]
  transfers between devices with their start and end apart: 17 -> 17, of which waited for: 16 -> 15; matrix products, arithmetic and copies ran while one was open for 6% -> 6% of each run, Pallas kernels for 0% -> 0%
where the time goes in v1:
time: 608 us; the launch traced here: 607 us
  waiting for transfers between devices  421 us (69%)
  blocking collectives  83.6 us (14%)
  matrix products  42.2 us (7%)
  other arithmetic  34.4 us (6%)
  between operations  17.4 us (3%)
  local copies, waits for them, and re-layouts  7.01 us (1%)
    psum x4, waiting for transfers between devices, head_total(): return lax.psum(partial_sum, 'tp')  120 us
    psum x1, waiting for transfers between devices, shards(): lax.psum(row_query.astype(jnp.bfloat16), 'ctx').astype(jnp.float32)  104 us
    reduce_scatter x1, waiting for transfers between devices, shards(): lax.psum_scatter(pair_terms, 'ctx', scatter_dimension=1, tiled=True)  31 us
    dot_general x20, matrix products, contract(): return jnp.einsum(pattern, left, right, preferred_element_type=jnp.float32)  29.8 us
    reduce_scatter x1, waiting for transfers between devices, shards(): lax.psum_scatter(grad_up.astype(jnp.bfloat16), 'fsdp', scatter_dimension=...  27.6 us
    reduce_scatter x1, waiting for transfers between devices, shards(): lax.psum_scatter(grad_gate.astype(jnp.bfloat16), 'fsdp', scatter_dimensio...  27.6 us
    reduce_scatter x1, waiting for transfers between devices, shards(): lax.psum_scatter(grad_down.astype(jnp.bfloat16), 'fsdp', scatter_dimensio...  27.4 us
    psum x1, blocking collectives, shards(): counted, squared = lax.psum((jnp.sum(weighting), placed), ('fsdp', 'ctx'))  21.2 us
  transfers between devices with their start and end apart: 17, of which 15 were waited for; matrix products, arithmetic and copies ran while one was open for 6% of the time, Pallas kernels for 0%

profile of v1, /device:TPU:0, one launch (start us, length us, event | category | flops | bytes accessed | tf_op | source)
XLA Modules:
  0.0 607.2 jit_solution(14014140105631144017)
XLA Ops:
  8.1 10.3 %all_gather.27 = bf16[1024,256]{1,0:T(8,128)(2,1)S(1)} all-gather(bf16[512,256]{1,0:T(8,128)(2,1)} %param.22), channel_id=1, replica_groups=mesh['fsdp'=2,'ctx'=4,'tp'=4] {'fsdp'}, dimensions={0}, use_global_device_ids=true | all-gather | bytes 786432 | tf_op jit(solution)/shard_map/all_gather | solution.py:67
  18.4 1.4 fusion.18
  19.9 8.3 %all_gather.26 = bf16[1024,256]{1,0:T(8,128)(2,1)S(1)} all-gather(bf16[512,256]{1,0:T(8,128)(2,1)} %param.21), channel_id=1, replica_groups=mesh['fsdp'=2,'ctx'=4,'tp'=4] {'fsdp'}, dimensions={0}, use_global_device_ids=true | all-gather | bytes 786432 | tf_op jit(solution)/shard_map/all_gather | solution.py:66
  28.2 1.7 convolution_convert_fusion.11
  31.2 11.1 %all_gather.29 = s32[1,1024]{1,0:T(1,128)S(1)} all-gather(s32[1,256]{1,0:T(1,128)S(1)} %copy-done.49), channel_id=1, replica_groups=mesh['fsdp'=2,'ctx'=4,'tp'=4] {'ctx'}, dimensions={1}, use_global_device_ids=true | all-gather | bytes 5120 | tf_op jit(solution)/shard_map/all_gather | solution.py:75
  42.3 8.4 %all_gather.31 = bf16[1024,256]{1,0:T(8,128)(2,1)S(1)} all-gather(bf16[512,256]{1,0:T(8,128)(2,1)S(1)} %copy-done.36), channel_id=1, replica_groups=mesh['fsdp'=2,'ctx'=4,'tp'=4] {'fsdp'}, dimensions={0}, use_global_device_ids=true | all-gather | bytes 786432 | tf_op jit(solution)/shard_map/all_gather | solution.py:65
  50.8 7.0 %all_gather.32 = bf16[256,1024]{1,0:T(8,128)(2,1)S(1)} all-gather(bf16[256,512]{1,0:T(8,128)(2,1)S(1)} %copy-done.37), channel_id=1, replica_groups=mesh['fsdp'=2,'ctx'=4,'tp'=4] {'fsdp'}, dimensions={1}, use_global_device_ids=true | all-gather | bytes 786432 | tf_op jit(solution)/shard_map/all_gather | solution.py:72
  58.6 3.8 all-gather.9.cloned.1.call-done
  62.4 1.3 fusion.60
  63.7 0.8 copy-done.11
  64.5 1.0 fusion.1
  65.5 1.5 fusion
  67.0 1.8 fusion.15
  69.4 1.3 fusion.61
  72.2 33.5 %all-reduce.12.cloned.1.call-done = f32[256,1024]{1,0:T(8,128)} async-done(((f32[256,1024]{1,0:T(8,128)}), f32[256,1024]{1,0:T(8,128)}) %all-reduce.12.cloned.1.call-update) | async-done | bytes 1048592 | tf_op jit(solution)/shard_map/psum | solution.py:36
  105.7 1.4 multiply_reduce_fusion.3
  107.4 2.1 fusion.13
  109.5 0.8 copy-done.28
  110.4 3.5 multiply_convert_fusion.3
  113.9 16.0 %all-gather.7.cloned.1.call-done = bf16[704,1024]{1,0:T(8,128)(2,1)} async-done(((bf16[704,512]{1,0:T(8,128)(2,1)}), bf16[704,1024]{1,0:T(8,128)(2,1)}) %all-gather.7.cloned.1.call-update) | async-done | bytes 1441808 | tf_op jit(solution)/shard_map/all_gather | solution.py:73
  129.9 3.0 fusion.62
  133.0 36.4 %all-reduce.14.cloned.1.call-done = f32[256,1024]{1,0:T(8,128)} async-done(((f32[256,1024]{1,0:T(8,128)}), f32[256,1024]{1,0:T(8,128)}) %all-reduce.14.cloned.1.call-update) | async-done | bytes 1048592 | tf_op jit(solution)/shard_map/psum | solution.py:36
  169.4 1.5 multiply_add_fusion
  171.0 2.7 multiply_convert_fusion.2
  174.6 3.0 convolution_add_fusion.2
  178.6 36.0 %all-reduce.16.cloned.1.call-done = f32[256,1024]{1,0:T(8,128)} async-done(((f32[256,1024]{1,0:T(8,128)}), f32[256,1024]{1,0:T(8,128)}) %all-reduce.16.cloned.1.call-update) | async-done | bytes 1048592 | tf_op jit(solution)/shard_map/psum | solution.py:36
  214.5 3.3 multiply_reduce_fusion.1
  219.3 1.5 copy-done.1
  221.0 1.9 multiply_reduce_fusion
  222.9 1.3 fusion.2
  224.2 1.4 multiply_convert_fusion
  226.2 1.5 maximum_bitcast_fusion
  227.7 1.8 fusion.14
  230.2 2.3 convolution_convert_fusion.6
  232.6 2.0 convolution_convert_fusion.3
  234.7 1.6 convolution_convert_fusion.1
  236.4 2.7 convolution_convert_fusion
  239.2 1.6 convolution_convert_fusion.2
  241.0 31.0 %reduce-scatter.9.cloned.1.call-done = f32[1,256,512]{1,2,0:T(8,128)} async-done(((f32[1,1024,512]{1,2,0:T(8,128)}), f32[1,256,512]{1,2,0:T(8,128)}) %reduce-scatter.9.cloned.1.call-update) | async-done | bytes 524304 | tf_op jit(solution)/shard_map/reduce_scatter | solution.py:187
  271.9 1.1 convert_bitcast_fusion.2
  273.0 1.2 convolution_convert_fusion.5
  274.4 1.2 convolution_convert_fusion.4
  276.4 1.3 convolution_add_fusion
  277.9 10.6 %reduce-scatter.11.cloned.1.call-done = bf16[512,256]{1,0:T(8,128)(2,1)} async-done(((bf16[1024,256]{1,0:T(8,128)(2,1)}), bf16[512,256]{1,0:T(8,128)(2,1)}) %reduce-scatter.11.cloned.1.call-update) | async-done | bytes 262160 | tf_op jit(solution)/shard_map/reduce_scatter | solution.py:206
  288.4 16.9 %reduce-scatter.17.cloned.1.call-done = bf16[256,512]{1,0:T(8,128)(2,1)} async-done(((bf16[256,1024]{1,0:T(8,128)(2,1)}), bf16[256,512]{1,0:T(8,128)(2,1)}) %reduce-scatter.17.cloned.1.call-update) | async-done | bytes 262160 | tf_op jit(solution)/shard_map/reduce_scatter | solution.py:229
  305.4 27.6 %reduce-scatter.19.cloned.1.call-done = bf16[512,704]{0,1:T(8,128)(2,1)} async-done(((bf16[1024,704]{0,1:T(8,128)(2,1)}), bf16[512,704]{0,1:T(8,128)(2,1)}) %reduce-scatter.19.cloned.1.call-update) | async-done | bytes 720912 | tf_op jit(solution)/shard_map/reduce_scatter | solution.py:215
  332.9 27.6 %reduce-scatter.21.cloned.1.call-done = bf16[512,704]{0,1:T(8,128)(2,1)} async-done(((bf16[1024,704]{0,1:T(8,128)(2,1)}), bf16[512,704]{0,1:T(8,128)(2,1)}) %reduce-scatter.21.cloned.1.call-update) | async-done | bytes 720912 | tf_op jit(solution)/shard_map/reduce_scatter | solution.py:218
  360.5 27.4 %reduce-scatter.23.cloned.1.call-done = bf16[704,512]{1,0:T(8,128)(2,1)} async-done(((bf16[704,1024]{1,0:T(8,128)(2,1)}), bf16[704,512]{1,0:T(8,128)(2,1)}) %reduce-scatter.23.cloned.1.call-update) | async-done | bytes 720912 | tf_op jit(solution)/shard_map/reduce_scatter | solution.py:232
  387.9 17.5 %reduce-scatter.13.cloned.1.call-done = bf16[512,256]{1,0:T(8,128)(2,1)} async-done(((bf16[1024,256]{1,0:T(8,128)(2,1)}), bf16[512,256]{1,0:T(8,128)(2,1)}) %reduce-scatter.13.cloned.1.call-update) | async-done | bytes 262160 | tf_op jit(solution)/shard_map/reduce_scatter | solution.py:209
  405.4 17.3 %reduce-scatter.15.cloned.1.call-done = bf16[512,256]{1,0:T(8,128)(2,1)} async-done(((bf16[1024,256]{1,0:T(8,128)(2,1)}), bf16[512,256]{1,0:T(8,128)(2,1)}) %reduce-scatter.15.cloned.1.call-update) | async-done | bytes 262160 | tf_op jit(solution)/shard_map/reduce_scatter | solution.py:212
  425.3 21.2 %all-reduce.2 = (f32[2]{0:T(128)S(1)}, f32[]{:T(128)}) all-reduce(f32[2]{0:T(128)S(1)} %compare_select_fusion, f32[]{:T(128)} %convert_reduce_fusion), channel_id=1, replica_groups=mesh['fsdp'=2,'ctx'=4,'tp'=4] {'fsdp','ctx'}, use_global_device_ids=true, to_apply=%region_7.8 | all-reduce | flops 3 | bytes 24 | tf_op jit(solution)/shard_map/psum | solution.py:138
  447.6 14.4 %all-reduce.18.cloned.1.call-done = f32[256,1024]{1,0:T(8,128)} async-done(((f32[256,1024]{1,0:T(8,128)}), f32[256,1024]{1,0:T(8,128)}) %all-reduce.18.cloned.1.call-update) | async-done | bytes 1048592 | tf_op jit(solution)/shard_map/psum | solution.py:36
  462.0 1.6 fusion.17
  463.6 4.9 all-reduce.5
  468.7 12.3 %all-reduce.3 = (bf16[512]{0:T(512)(128)(2,1)S(1)}, bf16[512]{0:T(512)(128)(2,1)S(1)}) all-reduce(bf16[512]{0:T(512)(128)(2,1)S(1)} %dynamic-slice.2, bf16[512]{0:T(512)(128)(2,1)S(1)} %dynamic-slice.4), channel_id=1, replica_groups=mesh['fsdp'=2,'ctx'=4,'tp'=4] {'ctx'}, use_global_device_ids=true, to_apply=%region_18.19 | all-reduce | flops 1024 | bytes 4096 | tf_op jit(solution)/shard_map/psum | solution.py:242
  482.1 2.5 fusion.25
  484.6 104.2 %all-reduce.20.cloned.1.call-done = (bf16[512,256]{1,0:T(8,128)(2,1)}, bf16[512,256]{1,0:T(8,128)(2,1)}, bf16[512,256]{1,0:T(8,128)(2,1)}, bf16[256,512]{1,0:T(8...) async-done(((bf16[512,256]{1,0:T(8,128)(2,1)}, bf16[512,256]{1,0:T(8,128)(2,1)}, bf16[512,256]{1,0:T(8,128)(2,1)}, ...) | async-done | bytes 3211280 | tf_op jit(solution)/shard_map/psum | solution.py:237
  588.9 1.9 convert_element_type.237
  590.7 1.8 convert_element_type.239
  592.5 1.8 convert_element_type.241
  594.4 1.8 convert_element_type.243
  596.2 1.3 convert_element_type.247
  597.5 1.3 convert_element_type.249
  598.8 1.3 convert_element_type.251
  (170 shorter events, 13.8 us)
Async XLA Ops:
  8.0 21.9 %copy-start.4 = (bf16[1,256,1024]{2,1,0:T(8,128)(2,1)S(1)}, bf16[1,256,1024]{2,1,0:T(8,128)(2,1)}, u32[]{:S(2)}) copy-start(bf16[1,256,1024]{2,1,0:T(8,128)(2,1)} %param.14) | copy-start | bytes 1572868
  8.0 21.9 %copy-start.39 = (f32[1024]{0:T(1024)S(1)}, f32[1024]{0:T(1024)}, u32[]{:S(2)}) copy-start(f32[1024]{0:T(1024)} %param.19) | copy-start | bytes 12292
  8.0 23.2 %copy-start.49 = (s32[1,256]{1,0:T(1,128)S(1)}, s32[1,256]{1,0:T(1,128)}, u32[]{:S(2)}) copy-start(s32[1,256]{1,0:T(1,128)} %param.18) | copy-start | bytes 3076
  8.0 34.3 %copy-start.36 = (bf16[512,256]{1,0:T(8,128)(2,1)S(1)}, bf16[512,256]{1,0:T(8,128)(2,1)}, u32[]{:S(2)}) copy-start(bf16[512,256]{1,0:T(8,128)(2,1)} %param.20) | copy-start | bytes 786436
  8.1 54.4 %all-gather.9.cloned.1.call-start = ((), (), s32[]{:S(2)}) async-start(), calls=%async_computation.22 | async-start | bytes 1310720 | tf_op jit(solution)/shard_map/all_gather | solution.py:92
  18.4 23.9 %copy-start.17 = (bf16[1024,256]{1,0:T(8,128)(2,1)}, bf16[1024,256]{1,0:T(8,128)(2,1)S(1)}, u32[]{:S(2)}) copy-start(bf16[1024,256]{1,0:T(8,128)(2,1)S(1)} %all_gather.27) | copy-start | bytes 1572868
  18.4 32.3 %copy-start.37 = (bf16[256,512]{1,0:T(8,128)(2,1)S(1)}, bf16[256,512]{1,0:T(8,128)(2,1)}, u32[]{:S(2)}) copy-start(bf16[256,512]{1,0:T(8,128)(2,1)} %param.23) | copy-start | bytes 786436
  19.9 11.4 %copy-start.43 = (f32[256]{0:T(256)}, f32[256]{0:T(256)S(1)}, u32[]{:S(2)}) copy-start(f32[256]{0:T(256)S(1)} %fusion.18) | copy-start | bytes 3076
  19.9 38.2 %copy-start.46 = (f32[256]{0:T(256)}, f32[256]{0:T(256)S(1)}, u32[]{:S(2)}) copy-start(f32[256]{0:T(256)S(1)} %fusion.44) | copy-start | bytes 3076
  31.2 74.6 %all-reduce.12.cloned.1.call-start = ((), (), s32[]{:S(2)}) async-start(), calls=%async_computation.8 | async-start | bytes 2097152 | tf_op jit(solution)/shard_map/psum | solution.py:36
  50.8 7.3 %copy-start.15 = (bf16[1024,256]{1,0:T(8,128)(2,1)}, bf16[1024,256]{1,0:T(8,128)(2,1)S(1)}, u32[]{:S(2)}) copy-start(bf16[1024,256]{1,0:T(8,128)(2,1)S(1)} %all_gather.31) | copy-start | bytes 1572868
  57.8 11.0 %copy-start.9 = (bf16[256,1024]{1,0:T(8,128)(2,1)}, bf16[256,1024]{1,0:T(8,128)(2,1)S(1)}, u32[]{:S(2)}) copy-start(bf16[256,1024]{1,0:T(8,128)(2,1)S(1)} %all_gather.32) | copy-start | bytes 1572868
  63.7 3.3 copy-start.30
  65.5 3.3 copy-start
  67.0 1.8 copy-start.41
  68.8 2.6 copy-start.52
  70.7 36.5 %copy-start.38 = (f32[1024]{0:T(1024)S(1)}, f32[1024]{0:T(1024)}, u32[]{:S(2)}) copy-start(f32[1024]{0:T(1024)} %param.24) | copy-start | bytes 12292
  70.8 36.7 %all-gather.5.cloned.1.call-start = ((), (), s32[]{:S(2)}) async-start(), calls=%async_computation.9 | async-start | bytes 2162688 | tf_op jit(solution)/shard_map/all_gather | solution.py:68
  71.3 58.6 %all-gather.7.cloned.1.call-start = ((), (), s32[]{:S(2)}) async-start(), calls=%async_computation.10 | async-start | bytes 2162688 | tf_op jit(solution)/shard_map/all_gather | solution.py:73
  71.4 38.2 %collective-permute-start = (bf16[512,704]{0,1:T(8,128)(2,1)S(1)}, bf16[512,704]{0,1:T(8,128)(2,1)}, u32[]{:S(2)}, u32[]{:S(2)}) collective-permute-start(bf16[512,704]{0,1:T(8,128)(2,1)S(1)} %copy-done.52), channel_id=1, source_target_pairs={{0,16},{16,0},{1,17},{17,1},{2,18},{18,2},{3,19},{19,3},{4,20},{20... | collective-permute-start | bytes 2162696 | tf_op jit(solution)/shard_map/ppermute | solution.py:13
  72.2 97.2 %all-reduce.14.cloned.1.call-start = ((), (), s32[]{:S(2)}) async-start(), calls=%async_computation.11 | async-start | bytes 2097152 | tf_op jit(solution)/shard_map/psum | solution.py:36
  107.2 6.7 %copy-start.45 = (f32[256]{0:T(256)}, f32[256]{0:T(256)S(1)}, u32[]{:S(2)}) copy-start(f32[256]{0:T(256)S(1)} %get-tuple-element.84) | copy-start | bytes 3076
  107.4 6.5 %copy-start.6 = (bf16[256,1024]{1,0:T(8,128)(2,1)}, bf16[256,1024]{1,0:T(8,128)(2,1)S(1)}, u32[]{:S(2)}) copy-start(bf16[256,1024]{1,0:T(8,128)(2,1)S(1)} %multiply_convert_fusion.1) | copy-start | bytes 1572868
  113.9 55.5 %copy-start.23 = (bf16[256,704]{0,1:T(8,128)(2,1)}, bf16[256,704]{0,1:T(8,128)(2,1)S(1)}, u32[]{:S(2)}) copy-start(bf16[256,704]{0,1:T(8,128)(2,1)S(1)} %get-tuple-element.93) | copy-start | bytes 1081348
  113.9 19.1 %copy-start.50 = (s32[1,256]{1,0:T(1,128)S(1)}, s32[1,256]{1,0:T(1,128)}, u32[]{:S(2)}) copy-start(s32[1,256]{1,0:T(1,128)} %param.17) | copy-start | bytes 3076
  113.9 55.5 %copy-start.14 = (bf16[1,256,1024]{2,1,0:T(8,128)(2,1)S(1)}, bf16[1,256,1024]{2,1,0:T(8,128)(2,1)}, u32[]{:S(2)}) copy-start(bf16[1,256,1024]{2,1,0:T(8,128)(2,1)} %param.16) | copy-start | bytes 1572868
  129.9 39.5 %copy-start.29 = (bf16[1,256,1024]{2,1,0:T(8,128)(2,1)S(1)}, bf16[1,256,1024]{2,1,0:T(8,128)(2,1)}, u32[]{:S(2)}) copy-start(bf16[1,256,1024]{2,1,0:T(8,128)(2,1)} %param.15) | copy-start | bytes 1572868
  132.9 81.6 %all-reduce.16.cloned.1.call-start = ((), (), s32[]{:S(2)}) async-start(), calls=%async_computation.12 | async-start | bytes 2097152 | tf_op jit(solution)/shard_map/psum | solution.py:36
  133.0 40.7 %copy-start.42 = (f32[1,256]{1,0:T(1,128)}, f32[1,256]{1,0:T(1,128)S(1)}, u32[]{:S(2)}) copy-start(f32[1,256]{1,0:T(1,128)S(1)} %convert_element_type.214) | copy-start | bytes 3076
  171.0 47.7 %copy-start.2 = (f32[256,1024]{1,0:T(8,128)}, f32[256,1024]{1,0:T(8,128)S(1)}, u32[]{:S(2)}) copy-start(f32[256,1024]{1,0:T(8,128)S(1)} %multiply_add_fusion) | copy-start | bytes 3145732
  171.0 2.8 copy-start.8
  171.0 3.6 copy-start.53
  174.6 40.0 %copy-start.12 = (f32[256,1024]{1,0:T(8,128)S(1)}, f32[256,1024]{1,0:T(8,128)}, u32[]{:S(2)}) copy-start(f32[256,1024]{1,0:T(8,128)} %all-reduce.14.cloned.1.call-done) | copy-start | bytes 3145732
  177.6 94.3 %reduce-scatter.9.cloned.1.call-start = ((), (), s32[]{:S(2)}) async-start(), calls=%async_computation.13 | async-start | bytes 2621440 | tf_op jit(solution)/shard_map/reduce_scatter | solution.py:187
  214.5 4.1 copy-start.13
  218.6 2.2 copy-start.1
  218.6 2.3 copy-start.31
  227.6 2.6 copy-start.40
  227.6 2.6 copy-start.47
  227.7 7.0 %copy-start.22 = (bf16[256,704]{0,1:T(8,128)(2,1)S(1)}, bf16[256,704]{0,1:T(8,128)(2,1)}, u32[]{:S(2)}) copy-start(bf16[256,704]{0,1:T(8,128)(2,1)} %copy-done.21) | copy-start | bytes 1081348
  227.7 60.8 %reduce-scatter.11.cloned.1.call-start = ((), (), s32[]{:S(2)}) async-start(), calls=%async_computation.15 | async-start | bytes 786432 | tf_op jit(solution)/shard_map/reduce_scatter | solution.py:206
  229.6 5.1 copy-start.7
  232.5 72.8 %reduce-scatter.17.cloned.1.call-start = ((), (), s32[]{:S(2)}) async-start(), calls=%async_computation.18 | async-start | bytes 786432 | tf_op jit(solution)/shard_map/reduce_scatter | solution.py:229
  234.6 98.3 %reduce-scatter.19.cloned.1.call-start = ((), (), s32[]{:S(2)}) async-start(), calls=%async_computation.19 | async-start | bytes 2162688 | tf_op jit(solution)/shard_map/reduce_scatter | solution.py:215
  236.3 2.9 copy-start.3
  236.3 2.9 copy-start.24
  236.4 124.1 %reduce-scatter.21.cloned.1.call-start = ((), (), s32[]{:S(2)}) async-start(), calls=%async_computation.20 | async-start | bytes 2162688 | tf_op jit(solution)/shard_map/reduce_scatter | solution.py:218
  239.2 33.8 %copy-start.5 = (bf16[1,256,1024]{2,1,0:T(8,128)(2,1)S(1)}, bf16[1,256,1024]{2,1,0:T(8,128)(2,1)}, u32[]{:S(2)}) copy-start(bf16[1,256,1024]{2,1,0:T(8,128)(2,1)} %param.14) | copy-start | bytes 1572868
  239.2 148.7 %reduce-scatter.23.cloned.1.call-start = ((), (), s32[]{:S(2)}) async-start(), calls=%async_computation.21 | async-start | bytes 2162688 | tf_op jit(solution)/shard_map/reduce_scatter | solution.py:232
  240.9 34.8 %copy-start.16 = (bf16[1024,256]{1,0:T(8,128)(2,1)S(1)}, bf16[1024,256]{1,0:T(8,128)(2,1)}, u32[]{:S(2)}) copy-start(bf16[1024,256]{1,0:T(8,128)(2,1)} %copy-done.15) | copy-start | bytes 1572868
  240.9 34.8 %copy-start.34 = (bf16[4,64,256]{2,1,0:T(8,128)(2,1)S(1)}, bf16[4,64,256]{2,1,0:T(8,128)(2,1)}, u32[]{:S(2)}) copy-start(bf16[4,64,256]{2,1,0:T(8,128)(2,1)} %copy-done.33) | copy-start | bytes 393220
  240.9 164.5 %reduce-scatter.13.cloned.1.call-start = ((), (), s32[]{:S(2)}) async-start(), calls=%async_computation.16 | async-start | bytes 786432 | tf_op jit(solution)/shard_map/reduce_scatter | solution.py:209
  273.0 3.0 copy-start.20
  274.3 2.1 copy-start.18
  274.3 148.4 %reduce-scatter.15.cloned.1.call-start = ((), (), s32[]{:S(2)}) async-start(), calls=%async_computation.17 | async-start | bytes 786432 | tf_op jit(solution)/shard_map/reduce_scatter | solution.py:212
  275.6 186.4 %all-reduce.18.cloned.1.call-start = ((), (), s32[]{:S(2)}) async-start(), calls=%async_computation.14 | async-start | bytes 2097152 | tf_op jit(solution)/shard_map/psum | solution.py:36
  276.4 146.3 %copy-start.54 = (u32[32]{0:T(128)S(1)}, u32[32]{0:T(128)}, u32[]{:S(2)}) copy-start(u32[32]{0:T(128)} %constant.97) | copy-start | bytes 388
  276.4 146.9 %copy-start.51 = (s32[1,256]{1,0:T(1,128)S(1)}, s32[1,256]{1,0:T(1,128)}, u32[]{:S(2)}) copy-start(s32[1,256]{1,0:T(1,128)} %param.17) | copy-start | bytes 3076
  277.8 185.8 %copy-start.48 = (bf16[1024]{0:T(1024)(128)(2,1)S(1)}, bf16[1024]{0:T(1024)(128)(2,1)}, u32[]{:S(2)}) copy-start(bf16[1024]{0:T(1024)(128)(2,1)} %get-tuple-element.56) | copy-start | bytes 6148
  277.8 204.3 %copy-start.44 = (f32[256]{0:T(256)S(1)}, f32[256]{0:T(256)}, u32[]{:S(2)}) copy-start(f32[256]{0:T(256)} %copy-done.43) | copy-start | bytes 3076
  277.8 311.1 %all-reduce.20.cloned.1.call-start = ((), (), s32[]{:S(2)}) async-start(), calls=%async_computation.23 | async-start | bytes 6422528 | tf_op jit(solution)/shard_map/psum | solution.py:237
  588.9 7.3 %copy-start.27 = (bf16[512,704]{0,1:T(8,128)(2,1)S(1)}, bf16[512,704]{0,1:T(8,128)(2,1)}, u32[]{:S(2)}) copy-start(bf16[512,704]{0,1:T(8,128)(2,1)} %get-tuple-element.79) | copy-start | bytes 2162692
  588.9 8.6 %copy-start.26 = (bf16[512,704]{0,1:T(8,128)(2,1)S(1)}, bf16[512,704]{0,1:T(8,128)(2,1)}, u32[]{:S(2)}) copy-start(bf16[512,704]{0,1:T(8,128)(2,1)} %get-tuple-element.80) | copy-start | bytes 2162692
  592.5 6.3 %copy-start.25 = (bf16[704,512]{1,0:T(8,128)(2,1)S(1)}, bf16[704,512]{1,0:T(8,128)(2,1)}, u32[]{:S(2)}) copy-start(bf16[704,512]{1,0:T(8,128)(2,1)} %get-tuple-element.81) | copy-start | bytes 2162692
  (9 other events, 8.9 us)
Sparse Core Ops, SparseCore 0:
  31.3 31.0 all-gather.8
  70.9 34.8 all-reduce.11
  133.1 36.2 all-reduce.13
  177.8 36.7 all-reduce.15
  227.8 44.0 reduce-scatter.8
  274.6 13.7 reduce-scatter.10
  290.7 14.6 reduce-scatter.16
  308.2 24.6 reduce-scatter.18
  335.7 24.6 reduce-scatter.20
  363.1 24.6 reduce-scatter.22
  390.7 14.6 reduce-scatter.12
  408.1 14.6 reduce-scatter.14
  425.7 36.2 all-reduce.17
  464.8 124.0 all-reduce.19
Sparse Core Ops, SparseCore 1:
  72.8 31.1 all-gather.4
  105.4 24.5 all-gather.6
